TPU v7x, 512 devices: a whole 4x8x8 slice. The times are simulated.
512 devices in a mesh: layer: 16 (over z, core), col: 32 (over x, y).
Axes of the slice: x: 4, y: 8, z: 8, core: 2. Of those that a mesh axis runs over, the one named last changes fastest.
Arguments:
- factors: bfloat16 [16, 32, 2048, 64], P('layer', 'col'), may hold values from -0.9 to 0.9
- cores: float32 [16, 64, 64], P('layer'), may hold values from -2 to 6, as said below
- tile_list: int32 [256, 2], P('col'), may hold values from 0 to 31, as said below
- probes: bfloat16 [2048, 256, 64], P(None, 'col'), may hold values from -6 to 6
Outputs:
- basis: float32 [2048, 256, 64], P('layer', 'col')
- update_right: float32 [2048, 256, 64], P('layer', 'col')
Inputs may be any that keep to these rules, and one draw needn't show every extreme that they name: `tile_list`: each row is a block row and a block column of a tile of the lower triangle: the first is not below the second. `cores`: each matrix is symmetric positive definite: a Gram matrix plus a positive diagonal.
All inputs are finite; a program needn't handle non-finite values.
Results may differ from a plain program's by a relative error of at most 0.02.
Values may be sent and summed in bfloat16 or wider, within the bound.
No kernel may reach another device: no remote copies, remote signals or barrier semaphores. Data moves between devices by JAX's collectives and lax.ppermute only.
A program may use at most 64 MiB of HBM per device.

v0:
```python
import math

import jax
import jax.numpy as jnp
from jax import lax
from jax.sharding import PartitionSpec as P


def local(factors, cores, tile_list, probes):
    highest = lax.Precision.HIGHEST
    tile_order = probes.shape[0]
    rank = probes.shape[2]
    gathered = lax.all_gather(factors, "col", axis=1, tiled=True)
    left_rows = jnp.take(gathered, tile_list[:, 0], axis=1)
    right_rows = jnp.take(gathered, tile_list[:, 1], axis=1)
    sketch = jnp.einsum("ktbr,bts->ktrs", right_rows, probes, preferred_element_type=jnp.float32)
    core_first = jnp.einsum("kar,ktrs->ktas", cores, sketch, precision=highest).astype(jnp.bfloat16)
    part_sample = jnp.einsum(
        "ktbr,ktrs->bts", left_rows, core_first, preferred_element_type=jnp.float32
    )
    share_rows = tile_order // lax.axis_size("layer")
    row_start = lax.axis_index("layer") * share_rows
    unit_matrix = jnp.eye(rank, dtype=jnp.float32)
    samples = lax.psum(part_sample.astype(jnp.bfloat16), "layer").astype(jnp.float32)
    gram = jnp.einsum("btr,bts->trs", samples, samples, precision=highest)
    chol = jnp.linalg.cholesky(gram)
    chol_inverse = jax.scipy.linalg.solve_triangular(
        chol, jnp.broadcast_to(unit_matrix, chol.shape), lower=True
    )
    ortho = jnp.einsum("btr,tsr->bts", samples, chol_inverse, precision=highest)
    ortho_half = ortho.astype(jnp.bfloat16)
    ortho_local = lax.dynamic_slice_in_dim(ortho, row_start, share_rows, 0)
    projected = jnp.einsum(
        "ktbr,bts->ktrs", left_rows, ortho_half, preferred_element_type=jnp.float32
    )
    core_second = jnp.einsum("kar,ktrs->ktas", cores, projected, precision=highest).astype(
        jnp.bfloat16
    )
    update_right = lax.psum_scatter(
        jnp.einsum(
            "ktbr,ktrs->bts", right_rows, core_second, preferred_element_type=jnp.float32
        ).astype(jnp.bfloat16),
        "layer",
        scatter_dimension=0,
        tiled=True,
    ).astype(jnp.float32)
    basis = ortho_local * math.sqrt(tile_order)
    return (basis, update_right)


def solution(mesh):
    placed = (
        P("layer", "col", None, None),
        P("layer", None, None),
        P("col", None),
        P(None, "col", None),
    )
    return jax.shard_map(
        local,
        mesh=mesh,
        in_specs=placed,
        out_specs=(P("layer", "col", None), P("layer", "col", None)),
        check_vma=False,
    )
```

profile of v0, /device:TPU:1, one launch (start us, length us, event | category | flops | bytes accessed | tf_op | source)
XLA Modules:
  0.0 426.5 jit_solution(14405846936379444862)
XLA Ops:
  7.2 0.0 copy-start
  7.2 0.0 all-gather.2.cloned.1.call-start
  7.2 0.7 all-gather.2.cloned.1.call-update
  7.9 0.0 all-reduce.2.cloned.1.call-start
  8.0 0.8 compare_and_fusion
  8.7 110.1 %all-gather.2.cloned.1.call-done = bf16[1,32,2048,64]{2,3,0,1:T(8,128)(2,1)} async-done(((bf16[1,1,2048,64]{2,3,0,1:T(8,128)(2,1)}), bf16[1,32,2048,64]{2,3,0,1:T(8,128)(2,1)}) %all-gather.2.cloned.1.call-update) | async-done | bytes 8388624 | tf_op jit(solution)/shard_map/all_gather | solution.py:13
  118.9 5.4 %gather_fusion.1 = bf16[8,2048,64]{1,2,0:T(8,128)(2,1)} fusion(bf16[32,2048,64]{1,2,0:T(8,128)(2,1)} %bitcast.93, s32[1024]{0:T(1024)S(1)} %get-tuple-element.9), kind=kCustom, calls=%fused_computation.1.clone | custom fusion | bytes 4194336 | tf_op jit(solution)/shard_map/jit(_take)/gather | solution.py:14
  124.2 5.4 %gather_fusion = bf16[8,2048,64]{1,2,0:T(8,128)(2,1)} fusion(bf16[32,2048,64]{1,2,0:T(8,128)(2,1)} %bitcast.94, s32[1024]{0:T(1024)S(1)} %get-tuple-element.10), kind=kCustom, calls=%fused_computation.clone | custom fusion | bytes 4194336 | tf_op jit(solution)/shard_map/jit(_take)/gather | solution.py:15
  129.7 0.0 copy-done
  129.7 0.0 copy-start.5
  129.7 0.0 copy-start.1
  129.7 2.5 fusion.6
  132.2 0.0 copy-done.5
  132.2 0.4 fusion.14
  132.6 0.0 copy-done.1
  132.6 2.1 fusion
  134.7 0.0 all-reduce.2.cloned.1.call-update
  134.7 0.0 reduce-scatter.4.cloned.1.call-start
  134.8 119.9 %all-reduce.2.cloned.1.call-done = bf16[2048,8,64]{0,2,1:T(8,128)(2,1)} async-done(((bf16[2048,8,64]{0,2,1:T(8,128)(2,1)}), bf16[2048,8,64]{0,2,1:T(8,128)(2,1)}) %all-reduce.2.cloned.1.call-update) | async-done | bytes 2097168 | tf_op jit(solution)/shard_map/psum | solution.py:24
  254.7 2.9 fusion.27
  257.6 0.1 copy.11
  257.8 46.9 %custom-call.8 = f32[8,64,64]{2,1,0:T(8,128)S(1)} custom-call(f32[8,64,64]{2,1,0:T(8,128)S(1)} %fusion.18), custom_call_target="Cholesky" | custom-call | tf_op jit(solution)/shard_map/jit(cholesky)/cholesky | solution.py:26
  304.7 0.1 compare_reduce_fusion
  304.9 0.1 select_bitcast_fusion
  305.0 39.3 %custom-call.9 = f32[8,1,64,64]{2,3,1,0:T(8,128)S(1)} custom-call(f32[8,1,64,64]{3,2,1,0:T(8,128)S(1)} %select_bitcast_fusion), custom_call_target="InvertDiagBlocksLowerTriangular" | custom-call | tf_op jit(solution)/shard_map/jit(_solve_triangular)/vmap()/triangular_solve | solution.py:27
  344.3 0.6 fusion.16
  344.9 0.0 copy-start.2
  344.9 3.5 fusion.28
  348.4 0.0 copy-done.2
  348.4 0.0 copy-start.4
  348.5 0.0 copy-start.3
  348.5 0.8 fusion.9
  349.3 1.3 copy-done.4
  350.6 0.4 fusion.15
  351.0 0.6 copy-done.3
  351.6 2.1 convolution_convert_fusion
  353.7 3.9 copy.17
  357.6 0.0 reduce-scatter.4.cloned.1.call-update
  357.6 1.7 multiply_bitcast_fusion
  359.3 58.9 %reduce-scatter.4.cloned.1.call-done = bf16[128,512]{1,0:T(8,128)(2,1)} async-done(((bf16[2048,512]{1,0:T(8,128)(2,1)}), bf16[128,512]{1,0:T(8,128)(2,1)}) %reduce-scatter.4.cloned.1.call-update) | async-done | bytes 131088
  418.2 1.0 copy.18
  419.3 0.7 convert_element_type.56
  (6 shorter events, 0.1 us)
Async XLA Ops:
  7.2 122.5 %copy-start = (bf16[2048,8,64]{0,2,1:T(8,128)(2,1)S(1)}, bf16[2048,8,64]{0,2,1:T(8,128)(2,1)}, u32[]{:S(2)}) copy-start(bf16[2048,8,64]{0,2,1:T(8,128)(2,1)} %param.9) | copy-start | bytes 6291460
  7.2 111.7 %all-gather.2.cloned.1.call-start = ((), (), s32[]{:S(2)}) async-start(), calls=%async_computation.1 | async-start | bytes 8650752 | tf_op jit(solution)/shard_map/all_gather | solution.py:13
  7.9 246.8 %all-reduce.2.cloned.1.call-start = ((), (), s32[]{:S(2)}) async-start(), calls=%async_computation.2 | async-start | bytes 4194304 | tf_op jit(solution)/shard_map/psum | solution.py:24
  129.7 2.5 copy-start.5
  129.7 2.9 copy-start.1
  134.7 283.5 %reduce-scatter.4.cloned.1.call-start = ((), (), s32[]{:S(2)}) async-start(), calls=%async_computation.3 | async-start | bytes 2228224
  344.9 3.5 copy-start.2
  348.4 2.1 copy-start.4
  348.5 3.1 copy-start.3
Sparse Core Ops, SparseCore 0:
  11.2 107.6 all-gather.1
  134.8 119.8 all-reduce.1
  357.7 60.4 reduce-scatter.3
where the time goes:
time: 429 us; the launch traced here: 427 us
  waiting for transfers between devices  290 us (68%)
  other arithmetic  89.7 us (21%)
  local copies, waits for them, and re-layouts  17.8 us (4%)
  matrix products  15.2 us (4%)
  between operations  13.9 us (3%)
    psum x1, waiting for transfers between devices, local(): lax.psum(part_sample.astype(jnp.bfloat16), 'layer').astype(jnp.float32)  120 us
    all_gather x1, waiting for transfers between devices, local(): gathered = lax.all_gather(factors, 'col', axis=1, tiled=True)  110 us
    unnamed x4, waiting for transfers between devices  59.7 us
    another operation x4, other arithmetic, local(): chol = jnp.linalg.cholesky(gram)  47.1 us
    another operation x3, other arithmetic, local(): jax.scipy.linalg.solve_triangular(chol, jnp.broadcast_to(unit_matrix, cho...  39.4 us
  transfers between devices with their start and end apart: 3, of which 3 were waited for; matrix products, arithmetic and copies ran while one was open for 1% of the time, Pallas kernels for 0%

commit v1 on v0

v1 whole, which is shorter than its diff:
```python
import math

import jax
import jax.numpy as jnp
from jax import lax
from jax.experimental import pallas as pl
from jax.experimental.pallas import tpu as pltpu
from jax.sharding import Mesh, PartitionSpec as P

F32 = jnp.float32
BF16 = jnp.bfloat16
HIGHEST = lax.Precision.HIGHEST

NZ = 8
NT = 8
RANK = 64
PANELS = 8
DEPTH = PANELS * RANK
ROWS = 256
HALF = 128


def nt_dot(a, b, precision=None):
    return lax.dot_general(
        a, b, (((1,), (1,)), ((), ())), precision=precision, preferred_element_type=F32
    )


def nn_dot(a, b, precision=None):
    return lax.dot_general(
        a, b, (((1,), (0,)), ((), ())), precision=precision, preferred_element_type=F32
    )


def split3(x):
    hi = x.astype(BF16)
    rest = x - hi.astype(F32)
    mid = rest.astype(BF16)
    low = (rest - mid.astype(F32)).astype(BF16)
    return hi, mid, low


def slice_kernel(f_ref, o_ref):
    o_ref[0] = f_ref[...]


def sketch_kernel(rows_ref, z_ref, f_ref, probe_ref, cores_ref, o_ref):
    o_ref[0] = nt_dot(probe_ref[0], f_ref[0]).astype(BF16)


def core_products(total, cores_ref):
    parts = []
    for k in range(PANELS):
        block = total[:, k * RANK:(k + 1) * RANK]
        parts.append(nt_dot(block, cores_ref[k], HIGHEST))
    return parts


def first_kernel(part_ref, cores_ref, o_ref):
    total = part_ref[0].astype(F32)
    for q in range(1, NZ):
        total = total + part_ref[q].astype(F32)
    parts = core_products(total, cores_ref)
    for k in range(PANELS):
        half = parts[k].astype(BF16)
        for q in range(NZ):
            o_ref[q, :, k * RANK:(k + 1) * RANK] = half


def sample_kernel(rows_ref, core_ref, f_ref, o_ref):
    o_ref[0] = nn_dot(core_ref[0], f_ref[0]).astype(BF16)


def gram_kernel(rows_ref, own_ref, other_ref, f_ref, o_ref):
    total = own_ref[0].astype(F32) + other_ref[0].astype(F32)
    gram = nt_dot(total, total, HIGHEST)
    hi = total.astype(BF16)
    low = (total - hi.astype(F32)).astype(BF16)
    both = nt_dot(jnp.concatenate([hi, low], axis=0), f_ref[0])
    o_ref[0, :, 0:DEPTH] = (both[0:RANK] + both[RANK:2 * RANK]).astype(BF16)
    one, two, three = split3(gram)
    o_ref[0, :, DEPTH:DEPTH + RANK] = one
    o_ref[0, :, DEPTH + RANK:DEPTH + 2 * RANK] = two
    o_ref[0, :, DEPTH + 2 * RANK:DEPTH + 3 * RANK] = three
    o_ref[0, :, DEPTH + 3 * RANK:DEPTH + 4 * RANK] = three


def inverse_factor(gram):
    row_id = lax.broadcasted_iota(jnp.int32, (RANK, RANK), 0)
    col_id = lax.broadcasted_iota(jnp.int32, (RANK, RANK), 1)
    unit = jnp.where(row_id == col_id, 1.0, 0.0).astype(F32)
    work = jnp.concatenate([gram, unit], axis=1)
    blocks = [work[8 * b:8 * b + 8, :] for b in range(RANK // 8)]
    sub = lax.broadcasted_iota(jnp.int32, (8, 2 * RANK), 0)
    scales = []
    for p in range(RANK):
        home, at = divmod(p, 8)
        row = blocks[home][at:at + 1, :]
        pivot = row[:, p:p + 1]
        scaled = row * (1.0 / pivot)
        for b in range(home, RANK // 8):
            col = jnp.broadcast_to(blocks[b][:, p:p + 1], (8, 2 * RANK))
            if b == home:
                col = jnp.where(sub > at, col, 0.0)
            blocks[b] = blocks[b] - col * scaled
    work = jnp.concatenate(blocks, axis=0)
    diag = jnp.sum(jnp.where(row_id == col_id, work[:, 0:RANK], 0.0), axis=1, keepdims=True)
    return work[:, RANK:2 * RANK] * (1.0 / jnp.sqrt(diag))


def second_kernel(part_ref, cores_ref, o_ref):
    total = part_ref[0, :, 0:DEPTH].astype(F32)
    for q in range(1, NZ):
        total = total + part_ref[q, :, 0:DEPTH].astype(F32)
    gram = jnp.zeros((RANK, RANK), F32)
    for q in range(NZ):
        one = part_ref[q, :, DEPTH:DEPTH + RANK].astype(F32)
        two = part_ref[q, :, DEPTH + RANK:DEPTH + 2 * RANK].astype(F32)
        three = part_ref[q, :, DEPTH + 2 * RANK:DEPTH + 3 * RANK].astype(F32)
        gram = gram + (one + (two + three))
    inverse = inverse_factor(gram)
    projected = nn_dot(inverse, total, HIGHEST)
    parts = core_products(projected, cores_ref)
    one, two, _ = split3(inverse)
    for q in range(NZ):
        for k in range(PANELS):
            o_ref[q, :, k * RANK:(k + 1) * RANK] = parts[k].astype(BF16)
        o_ref[q, :, DEPTH:DEPTH + RANK] = one
        o_ref[q, :, DEPTH + RANK:DEPTH + 2 * RANK] = two


def final_kernel(rows_ref, side_ref, core_ref, own_ref, other_ref, f_ref, basis_ref, keep_ref, send_ref):
    inverse = core_ref[0, :, DEPTH:DEPTH + RANK].astype(F32)
    inverse = inverse + core_ref[0, :, DEPTH + RANK:DEPTH + 2 * RANK].astype(F32)
    total = own_ref[0].astype(F32) + other_ref[0].astype(F32)
    basis_ref[0] = nn_dot(inverse, total, HIGHEST) * math.sqrt(2048.0)
    part = nn_dot(core_ref[0, :, 0:DEPTH], f_ref[0])
    first, last = part[:, 0:HALF], part[:, HALF:ROWS]
    upper = side_ref[0] == 1
    keep_ref[0] = jnp.where(upper, last, first)
    send_ref[0] = jnp.where(upper, first, last).astype(BF16)


def in_hbm(x):
    return pltpu.with_memory_space_constraint(x, pltpu.HBM)


def local(factors, cores, tile_list, probes):
    swap = [(0, 1), (1, 0)]
    z = lax.axis_index("z").astype(jnp.int32).reshape(1)
    side = lax.axis_index("core").astype(jnp.int32).reshape(1)
    row_first = tile_list[:, 0].astype(jnp.int32)
    row_second = tile_list[:, 1].astype(jnp.int32)
    params = pltpu.CompilerParams(vmem_limit_bytes=32 * 1024 * 1024)

    def call(kernel, scalars, out_shape, in_specs, out_specs, *args):
        return pl.pallas_call(
            kernel,
            out_shape=out_shape,
            grid_spec=pltpu.PrefetchScalarGridSpec(
                num_scalar_prefetch=len(scalars), grid=(NT,), in_specs=in_specs, out_specs=out_specs
            ),
            compiler_params=params,
        )(*scalars, *args)

    def tile_spec(rows, lanes):
        return pl.BlockSpec((1, rows, lanes), lambda t, *_: (t, 0, 0))

    gathered_spec = pl.BlockSpec((1, DEPTH, ROWS), lambda t, rows, *_: (rows[t], 0, 0))

    def exchange(x):
        return lax.all_to_all(x, "z", 0, 0, tiled=True)

    mine = jnp.transpose(factors[0, 0], (1, 0))
    sliced = call(
        slice_kernel,
        (),
        jax.ShapeDtypeStruct((NZ, RANK, ROWS), BF16),
        [pl.BlockSpec((RANK, ROWS), lambda t: (0, t))],
        pl.BlockSpec((1, RANK, ROWS), lambda t: (t, 0, 0)),
        mine,
    )
    panels = exchange(sliced).reshape(DEPTH, ROWS)
    gathered = in_hbm(lax.all_gather(panels, ("x", "y"), axis=0, tiled=False))
    core, _ = lax.optimization_barrier((cores[0], panels))
    all_cores = lax.all_gather(core, "z", axis=0, tiled=False)

    probe = in_hbm(jnp.transpose(probes, (1, 2, 0)))
    sketch = call(
        sketch_kernel,
        (row_second, z),
        jax.ShapeDtypeStruct((NT, RANK, DEPTH), BF16),
        [
            gathered_spec,
            pl.BlockSpec((1, RANK, ROWS), lambda t, rows, zz: (t, 0, zz[0])),
            pl.BlockSpec(memory_space=pl.ANY),
        ],
        tile_spec(RANK, DEPTH),
        gathered,
        probe,
        all_cores,
    )
    sketch = exchange(sketch)
    first = pl.pallas_call(
        first_kernel, out_shape=jax.ShapeDtypeStruct((NZ, RANK, DEPTH), BF16), compiler_params=params
    )(sketch, all_cores)
    first = exchange(first)
    own = call(
        sample_kernel,
        (row_first,),
        jax.ShapeDtypeStruct((NT, RANK, ROWS), BF16),
        [tile_spec(RANK, DEPTH), gathered_spec],
        tile_spec(RANK, ROWS),
        first,
        gathered,
    )
    other = lax.ppermute(own, "core", swap)
    wide = DEPTH + 4 * RANK
    stacked = call(
        gram_kernel,
        (row_first,),
        jax.ShapeDtypeStruct((NT, RANK, wide), BF16),
        [tile_spec(RANK, ROWS), tile_spec(RANK, ROWS), gathered_spec],
        tile_spec(RANK, wide),
        own,
        other,
        gathered,
    )
    stacked = exchange(stacked)
    wide = DEPTH + 2 * RANK
    second = pl.pallas_call(
        second_kernel, out_shape=jax.ShapeDtypeStruct((NZ, RANK, wide), BF16), compiler_params=params
    )(stacked, all_cores)
    second = exchange(second)
    half_spec = pl.BlockSpec((1, RANK, HALF), lambda t, rows, ss: (t, 0, ss[0]))
    basis, keep, send = call(
        final_kernel,
        (row_second, side),
        (
            jax.ShapeDtypeStruct((NT, RANK, HALF), F32),
            jax.ShapeDtypeStruct((NT, RANK, HALF), F32),
            jax.ShapeDtypeStruct((NT, RANK, HALF), BF16),
        ),
        [tile_spec(RANK, wide), half_spec, half_spec, gathered_spec],
        (tile_spec(RANK, HALF), tile_spec(RANK, HALF), tile_spec(RANK, HALF)),
        second,
        own,
        other,
        gathered,
    )
    update = keep + lax.ppermute(send, "core", swap).astype(F32)
    return jnp.transpose(basis, (2, 0, 1)), jnp.transpose(update, (2, 0, 1))


def solution(mesh):
    fine = Mesh(mesh.devices.reshape(8, 2, 4, 8), ("z", "core", "x", "y"))
    layer, col = ("z", "core"), ("x", "y")
    placed = (
        P(layer, col, None, None),
        P(layer, None, None),
        P(col, None),
        P(None, col, None),
    )
    return jax.shard_map(
        local,
        mesh=fine,
        in_specs=placed,
        out_specs=(P(layer, col, None), P(layer, col, None)),
        check_vma=False,
    )
```

time: 429 us -> 270 us (0.63)
  waiting for transfers between devices: 290 us -> 103 us
  blocking collectives: 0 us -> 106 us
  other arithmetic: 89.7 us -> 0.73 us
  Pallas kernels: 0 us -> 31.8 us
  local copies, waits for them, and re-layouts: 17.8 us -> 1.7 us
  matrix products: 15.2 us -> 0 us
  starting transfers between devices: 0.12 us -> 11.9 us
    psum x1 -> x0, waiting for transfers between devices: 120 us -> none  [local(): lax.psum(part_sample.astype(jnp.bfloat16), 'layer').astype(jnp.float32)]
    all_to_all x0 -> x4, blocking collectives: none -> 86.8 us  [exchange(): return lax.all_to_all(x, 'z', 0, 0, tiled=True)]
    another operation x7 -> x0, other arithmetic: 86.5 us -> none  [the longest x4 47.1 us: local(): chol = jnp.linalg.cholesky(gram)]
    unnamed x4 -> x1, waiting for transfers between devices: 59.7 us -> 0.02 us
    pallas_call x0 -> x7, Pallas kernels: none -> 31.8 us  [the longest x5 23.7 us: call(): pl.pallas_call(kernel, out_shape=out_shape, grid_spec=pltpu.PrefetchScala...]
    all_gather x1, waiting for transfers between devices: 110 us -> 80.1 us  [local(): gathered = in_hbm(lax.all_gather(panels, ('x', 'y'), axis=0, tiled=False))]
    all_to_all x0 -> x1, waiting for transfers between devices: none -> 20.7 us  [exchange(): return lax.all_to_all(x, 'z', 0, 0, tiled=True)]
    all_gather x0 -> x1, blocking collectives: none -> 19.3 us  [local(): all_cores = lax.all_gather(core, 'z', axis=0, tiled=False)]
  transfers between devices with their start and end apart: 3 -> 4, of which waited for: 3 -> 4; matrix products, arithmetic and copies ran while one was open for 1% -> 0% of each run, Pallas kernels for 0% -> 0%
where the time goes in v1:
time: 270 us; the launch traced here: 269 us
  blocking collectives  106 us (39%)
  waiting for transfers between devices  103 us (38%)
  Pallas kernels  31.8 us (12%)
  between operations  14.1 us (5%)
  starting transfers between devices  11.9 us (4%)
    all_to_all x4, blocking collectives, exchange(): return lax.all_to_all(x, 'z', 0, 0, tiled=True)  86.8 us
    all_gather x1, waiting for transfers between devices, local(): gathered = in_hbm(lax.all_gather(panels, ('x', 'y'), axis=0, tiled=False))  80.1 us
    pallas_call x5, Pallas kernels, call(): pl.pallas_call(kernel, out_shape=out_shape, grid_spec=pltpu.PrefetchScala...  23.7 us
    all_to_all x1, waiting for transfers between devices, exchange(): return lax.all_to_all(x, 'z', 0, 0, tiled=True)  20.7 us
    all_gather x1, blocking collectives, local(): all_cores = lax.all_gather(core, 'z', axis=0, tiled=False)  19.3 us
    pallas_call x1, Pallas kernels, local(): pl.pallas_call(second_kernel, out_shape=jax.ShapeDtypeStruct((NZ, RANK, w...  7.45 us
    ppermute x1, starting transfers between devices, local(): other = lax.ppermute(own, 'core', swap)  5.91 us
  transfers between devices with their start and end apart: 4, of which 4 were waited for; matrix products, arithmetic and copies ran while one was open for 0% of the time, Pallas kernels for 0%

profile of v1, /device:TPU:1, one launch (start us, length us, event | category | flops | bytes accessed | tf_op | source)
XLA Modules:
  0.0 269.2 jit_solution(13740596812625214123)
XLA Ops:
  7.2 0.0 all-gather.3.cloned.1.call-start
  7.2 0.0 copy-start
  7.2 0.9 copy-done
  8.2 0.2 shard_map.59
  8.4 21.3 %all_to_all.25 = bf16[8,64,256]{2,1,0:T(8,128)(2,1)} all-to-all(bf16[8,64,256]{2,1,0:T(8,128)(2,1)S(1)} %shard_map.59), channel_id=1, replica_groups=mesh['z'=8,'core'=2,'x'=4,'y'=8] {'z'}, dimensions={0} | all-to-all | bytes 524288 | tf_op jit(solution)/shard_map/all_to_all | solution.py:172
  29.6 0.0 all-gather.3.cloned.1.call-update
  29.7 19.3 %all-gather = f32[512,64]{1,0:T(8,128)S(1)} all-gather(f32[64,64]{1,0:T(8,128)} %bitcast.22), channel_id=2, replica_groups=mesh['z'=8,'core'=2,'x'=4,'y'=8] {'z'}, dimensions={0}, use_global_device_ids=true | all-gather | bytes 147456 | tf_op jit(solution)/shard_map/all_gather | solution.py:186
  49.0 0.8 slice_bitcast_fusion
  49.7 80.1 %all-gather.3.cloned.1.call-done.f_ref = bf16[32,512,256]{2,1,0:T(8,128)(2,1)} async-done(((bf16[1,512,256]{2,1,0:T(8,128)(2,1)}), bf16[32,512,256]{2,1,0:T(8,128)(2,1)}) %all-gather.3.cloned.1.call-update) | async-done | bytes 8388624 | tf_op jit(solution)/shard_map/all_gather | solution.py:184
  129.8 5.5 %shard_map.60 = bf16[8,64,512]{2,1,0:T(8,128)(2,1)S(1)} custom-call(s32[8]{0:T(128)S(1)} %get-tuple-element.9.rows_ref, s32[1]{0:T(128)} %bitcast.3.z_ref, bf16[32,512,256]{2,1,0:T(8,128)(2,1)} %all-gather.3.cloned.1.call-done.f_ref, bf16[8,64,2048]{2,1,0:T(8,128)(2,1)} %bitcast.20, f32[8,64,64]{2,1,0:T(8,128)S(1)} %bitcast.16), custom_call_target="tpu_custom_call" | custom-call | tf_op jit(solution)/shard_map/pallas_call | solution.py:157
  135.3 22.1 %all_to_all.26.part_ref = bf16[8,64,512]{2,1,0:T(8,128)(2,1)S(1)} all-to-all(bf16[8,64,512]{2,1,0:T(8,128)(2,1)S(1)} %shard_map.60), channel_id=1, replica_groups=mesh['z'=8,'core'=2,'x'=4,'y'=8] {'z'}, dimensions={0} | all-to-all | bytes 1048576 | tf_op jit(solution)/shard_map/all_to_all | solution.py:172
  157.4 0.7 shard_map.61
  158.1 17.5 %all_to_all.27.core_ref = bf16[8,64,512]{2,1,0:T(8,128)(2,1)S(1)} all-to-all(bf16[8,64,512]{2,1,0:T(8,128)(2,1)S(1)} %shard_map.61), channel_id=1, replica_groups=mesh['z'=8,'core'=2,'x'=4,'y'=8] {'z'}, dimensions={0} | all-to-all | bytes 1048576 | tf_op jit(solution)/shard_map/all_to_all | solution.py:172
  175.6 5.3 %shard_map.62.own_ref = bf16[8,64,256]{2,1,0:T(8,128)(2,1)S(1)} custom-call(s32[8]{0:T(128)S(1)} %get-tuple-element.8.rows_ref, bf16[8,64,512]{2,1,0:T(8,128)(2,1)S(1)} %all_to_all.27.core_ref, bf16[32,512,256]{2,1,0:T(8,128)(2,1)} %all-gather.3.cloned.1.call-done.f_ref), custom_call_target="tpu_custom_call" | custom-call | tf_op jit(solution)/shard_map/pallas_call | solution.py:157
  180.8 5.9 %collective-permute-start = (bf16[8,64,256]{2,1,0:T(8,128)(2,1)S(1)}, bf16[8,64,256]{2,1,0:T(8,128)(2,1)S(1)}, u32[]{:S(2)}, u32[]{:S(2)}) collective-permute-start(bf16[8,64,256]{2,1,0:T(8,128)(2,1)S(1)} %shard_map.62.own_ref), channel_id=1, source_target_pairs={{0,32},{32,0},{1,33},{33,1},{2,34},{34,2},{3,35},{35,3},{4,36},{36... | collective-permute-start | bytes 786440 | tf_op jit(solution)/shard_map/ppermute | solution.py:217
  186.8 1.1 collective-permute-done.other_ref
  187.9 6.0 %shard_map.63 = bf16[8,64,768]{2,1,0:T(8,128)(2,1)S(1)} custom-call(s32[8]{0:T(128)S(1)} %get-tuple-element.8.rows_ref, bf16[8,64,256]{2,1,0:T(8,128)(2,1)S(1)} %shard_map.62.own_ref, bf16[8,64,256]{2,1,0:T(8,128)(2,1)S(1)} %collective-permute-done.other_ref, bf16[32,512,256]{2,1,0:T(8,128)(2,1)} %all-gather.3.cloned.1.call-done.f_ref), custom_call_target="tpu_custom_call" | custom-call | tf_op jit(solution)/shard_map/pallas_call | solution.py:157
  193.9 26.0 %all_to_all.28.part_ref = bf16[8,64,768]{2,1,0:T(8,128)(2,1)S(1)} all-to-all(bf16[8,64,768]{2,1,0:T(8,128)(2,1)S(1)} %shard_map.63), channel_id=1, replica_groups=mesh['z'=8,'core'=2,'x'=4,'y'=8] {'z'}, dimensions={0} | all-to-all | bytes 1572864 | tf_op jit(solution)/shard_map/all_to_all | solution.py:172
  219.9 7.5 %shard_map.64 = bf16[8,64,640]{2,1,0:T(8,128)(2,1)} custom-call(bf16[8,64,768]{2,1,0:T(8,128)(2,1)S(1)} %all_to_all.28.part_ref, f32[8,64,64]{2,1,0:T(8,128)S(1)} %bitcast.18), custom_call_target="tpu_custom_call" | custom-call | tf_op jit(solution)/shard_map/pallas_call | solution.py:231
  227.3 3.5 %all-to-all-start.4 = ((bf16[8,64,640]{2,1,0:T(8,128)(2,1)}), bf16[8,64,640]{2,1,0:T(8,128)(2,1)S(1)}, u32[]{:S(2)}, u32[]{:S(2)}) async-start(bf16[8,64,640]{2,1,0:T(8,128)(2,1)} %shard_map.64), calls=%async_computation.4 | async-start | bytes 1310720 | tf_op jit(solution)/shard_map/all_to_all | solution.py:172
  230.9 20.7 %all-to-all-done.4.core_ref = bf16[8,64,640]{2,1,0:T(8,128)(2,1)S(1)} async-done(((bf16[8,64,640]{2,1,0:T(8,128)(2,1)}), bf16[8,64,640]{2,1,0:T(8,128)(2,1)S(1)}, u32[]{:S(2)}, u32[]{:S(2)}) %all-to-all-start.4) | async-done | bytes 655392 | tf_op jit(solution)/shard_map/all_to_all | solution.py:172
  251.6 6.7 %shard_map.65 = (f32[8,64,128]{2,1,0:T(8,128)}, f32[8,64,128]{2,1,0:T(8,128)S(1)}, bf16[8,64,128]{2,1,0:T(8,128)(2,1)S(1)}) custom-call(s32[8]{0:T(128)S(1)} %get-tuple-element.9.rows_ref, s32[1]{0:T(128)} %bitcast.1.side_ref, bf16[8,64,640]{2,1,0:T(8,128)(2,1)S(1)} %all-to-all-done.4.core_ref, bf16[8,64,256]{2,1,0:T(8,128)(2,1)S(1)} %shard_map.62.own_ref, ...), custom_call_target="tpu_custom_call" | custom-call | tf_op jit(solution)/shard_map/pallas_call | solution.py:157
  258.3 2.4 collective-permute-start.1
  260.7 1.0 collective-permute-done.1
  261.7 0.7 add_bitcast_fusion
Async XLA Ops:
  7.2 122.7 %all-gather.3.cloned.1.call-start = ((), (), s32[]{:S(2)}) async-start(), calls=%async_computation.5 | async-start | bytes 8650752 | tf_op jit(solution)/shard_map/all_gather | solution.py:184
  7.2 1.0 copy-start
  180.8 7.1 %collective-permute-start = (bf16[8,64,256]{2,1,0:T(8,128)(2,1)S(1)}, bf16[8,64,256]{2,1,0:T(8,128)(2,1)S(1)}, u32[]{:S(2)}, u32[]{:S(2)}) collective-permute-start(bf16[8,64,256]{2,1,0:T(8,128)(2,1)S(1)} %shard_map.62.own_ref), channel_id=1, source_target_pairs={{0,32},{32,0},{1,33},{33,1},{2,34},{34,2},{3,35},{35,3},{4,36},{36... | collective-permute-start | bytes 786440 | tf_op jit(solution)/shard_map/ppermute | solution.py:217
  227.3 24.2 %all-to-all-start.4 = ((bf16[8,64,640]{2,1,0:T(8,128)(2,1)}), bf16[8,64,640]{2,1,0:T(8,128)(2,1)S(1)}, u32[]{:S(2)}, u32[]{:S(2)}) async-start(bf16[8,64,640]{2,1,0:T(8,128)(2,1)} %shard_map.64), calls=%async_computation.4 | async-start | bytes 1310720 | tf_op jit(solution)/shard_map/all_to_all | solution.py:172
  258.3 3.4 %collective-permute-start.1 = (bf16[8,64,128]{2,1,0:T(8,128)(2,1)S(1)}, bf16[8,64,128]{2,1,0:T(8,128)(2,1)S(1)}, u32[]{:S(2)}, u32[]{:S(2)}) collective-permute-start(bf16[8,64,128]{2,1,0:T(8,128)(2,1)S(1)} %get-tuple-element.7), channel_id=1, source_target_pairs={{0,32},{32,0},{1,33},{33,1},{2,34},{34,2},{3,35},{35,3},{4,36},{36... | collective-permute-start | bytes 393224 | tf_op jit(solution)/shard_map/ppermute | solution.py:251
Sparse Core Ops, SparseCore 0:
  29.8 100.0 all-gather.2

commit v2 on v1

v2 whole, which is shorter than its diff:
```python
import math

import jax
import jax.numpy as jnp
from jax import lax
from jax.experimental import pallas as pl
from jax.experimental.pallas import tpu as pltpu
from jax.sharding import Mesh, PartitionSpec as P

F32 = jnp.float32
BF16 = jnp.bfloat16
HIGHEST = lax.Precision.HIGHEST

NZ = 8
NT = 8
RANK = 64
PANELS = 8
DEPTH = PANELS * RANK
ROWS = 256
HALF = 128


def nt_dot(a, b, precision=None):
    return lax.dot_general(
        a, b, (((1,), (1,)), ((), ())), precision=precision, preferred_element_type=F32
    )


def nn_dot(a, b, precision=None):
    return lax.dot_general(
        a, b, (((1,), (0,)), ((), ())), precision=precision, preferred_element_type=F32
    )


def split3(x):
    hi = x.astype(BF16)
    rest = x - hi.astype(F32)
    mid = rest.astype(BF16)
    low = (rest - mid.astype(F32)).astype(BF16)
    return hi, mid, low


def slice_kernel(f_ref, o_ref):
    o_ref[0] = f_ref[...]


def sketch_kernel(first_ref, second_ref, z_ref, f_ref, probe_ref, cores_ref, o_ref, left_ref, right_ref,
                  slot_ref, sem_right, sem_left, sem_probe):
    start = pl.multiple_of(z_ref[0] * ROWS, ROWS)
    rights, probes, lefts = [], [], []
    for t in range(NT):
        rights.append(pltpu.make_async_copy(f_ref.at[second_ref[t]], right_ref.at[t], sem_right.at[t]))
        probes.append(
            pltpu.make_async_copy(probe_ref.at[t, :, pl.ds(start, ROWS)], slot_ref.at[t], sem_probe.at[t])
        )
        lefts.append(pltpu.make_async_copy(f_ref.at[first_ref[t]], left_ref.at[t], sem_left.at[t]))
    for t in range(NT):
        rights[t].start()
        probes[t].start()
    for t in range(NT):
        lefts[t].start()
    for t in range(NT):
        rights[t].wait()
        probes[t].wait()
        o_ref[t] = nt_dot(slot_ref[t], right_ref[t]).astype(BF16)
    for t in range(NT):
        lefts[t].wait()


def core_products(total, cores_ref):
    parts = []
    for k in range(PANELS):
        block = total[:, k * RANK:(k + 1) * RANK]
        parts.append(nt_dot(block, cores_ref[k], HIGHEST))
    return parts


def first_kernel(part_ref, cores_ref, o_ref):
    total = part_ref[0].astype(F32)
    for q in range(1, NZ):
        total = total + part_ref[q].astype(F32)
    parts = core_products(total, cores_ref)
    for k in range(PANELS):
        half = parts[k].astype(BF16)
        for q in range(NZ):
            o_ref[q, :, k * RANK:(k + 1) * RANK] = half


def sample_kernel(core_ref, f_ref, o_ref):
    for t in range(NT):
        o_ref[t] = nn_dot(core_ref[t], f_ref[t]).astype(BF16)


def pack_gram(gram):
    row = lax.broadcasted_iota(jnp.int32, (RANK, RANK), 0)
    col = lax.broadcasted_iota(jnp.int32, (RANK, RANK), 1)
    one, two, three = (part.astype(F32) for part in split3(gram))
    diag = jnp.sum(jnp.where(row == col, two, 0.0), axis=1, keepdims=True)
    last = jnp.sum(jnp.where((row == RANK - 1) & (col == RANK - 1), two, 0.0), axis=(0, 1), keepdims=True)
    upper = jnp.where(col == row + 1, diag, 0.0)
    upper = jnp.where((row == 0) & (col == RANK - 1), last, upper)
    return jnp.where(col <= row, one, jnp.transpose(two)), jnp.where(col <= row, three, upper)


def unpack_gram(left, right):
    row = lax.broadcasted_iota(jnp.int32, (RANK, RANK), 0)
    col = lax.broadcasted_iota(jnp.int32, (RANK, RANK), 1)
    corner = (row == 0) & (col == RANK - 1)
    last = jnp.sum(jnp.where(corner, right, 0.0), axis=(0, 1), keepdims=True)
    diag = jnp.sum(jnp.where(col == row + 1, right, 0.0), axis=1, keepdims=True)
    two_diag = jnp.where((row == col) & (row < RANK - 1), diag, 0.0)
    two_diag = jnp.where((row == RANK - 1) & (col == RANK - 1), last, two_diag)
    lower = col <= row
    one = jnp.where(lower, left, 0.0)
    three = jnp.where(lower, right, 0.0)
    two = jnp.where(col > row, left, 0.0)
    strict = jnp.where(col < row, one, 0.0) + jnp.where(col < row, three, 0.0)
    full_diag = jnp.where(row == col, one + (three + two_diag), 0.0)
    below = strict + jnp.where(col < row, jnp.transpose(two), 0.0)
    return below + full_diag + jnp.transpose(below)


def gram_kernel(own_ref, other_ref, f_ref, o_ref):
    for t in range(NT):
        total = own_ref[t].astype(F32) + other_ref[t].astype(F32)
        gram = nt_dot(total, total, HIGHEST)
        hi = total.astype(BF16)
        low = (total - hi.astype(F32)).astype(BF16)
        both = nt_dot(jnp.concatenate([hi, low], axis=0), f_ref[t])
        o_ref[t, :, 0:DEPTH] = (both[0:RANK] + both[RANK:2 * RANK]).astype(BF16)
        left, right = pack_gram(gram)
        o_ref[t, :, DEPTH:DEPTH + 2 * RANK] = jnp.concatenate([left, right], axis=1).astype(BF16)


def inverse_factor(gram):
    row_id = lax.broadcasted_iota(jnp.int32, (RANK, RANK), 0)
    col_id = lax.broadcasted_iota(jnp.int32, (RANK, RANK), 1)
    unit = jnp.where(row_id == col_id, 1.0, 0.0).astype(F32)
    work = jnp.concatenate([gram, unit], axis=1)
    blocks = [work[8 * b:8 * b + 8, :] for b in range(RANK // 8)]
    sub = lax.broadcasted_iota(jnp.int32, (8, 2 * RANK), 0)
    scales = []
    for p in range(RANK):
        home, at = divmod(p, 8)
        row = blocks[home][at:at + 1, :]
        pivot = row[:, p:p + 1]
        scaled = row * (1.0 / pivot)
        for b in range(home, RANK // 8):
            col = jnp.broadcast_to(blocks[b][:, p:p + 1], (8, 2 * RANK))
            if b == home:
                col = jnp.where(sub > at, col, 0.0)
            blocks[b] = blocks[b] - col * scaled
    work = jnp.concatenate(blocks, axis=0)
    diag = jnp.sum(jnp.where(row_id == col_id, work[:, 0:RANK], 0.0), axis=1, keepdims=True)
    return work[:, RANK:2 * RANK] * (1.0 / jnp.sqrt(diag))


def second_kernel(part_ref, cores_ref, o_ref):
    total = part_ref[0, :, 0:DEPTH].astype(F32)
    for q in range(1, NZ):
        total = total + part_ref[q, :, 0:DEPTH].astype(F32)
    packed = part_ref[0, :, DEPTH:DEPTH + 2 * RANK].astype(F32)
    for q in range(1, NZ):
        packed = packed + part_ref[q, :, DEPTH:DEPTH + 2 * RANK].astype(F32)
    gram = unpack_gram(packed[:, 0:RANK], packed[:, RANK:2 * RANK])
    inverse = inverse_factor(gram)
    projected = nn_dot(inverse, total, HIGHEST)
    parts = core_products(projected, cores_ref)
    one, two, _ = split3(inverse)
    for q in range(NZ):
        for k in range(PANELS):
            o_ref[q, :, k * RANK:(k + 1) * RANK] = parts[k].astype(BF16)
        o_ref[q, :, DEPTH:DEPTH + RANK] = one
        o_ref[q, :, DEPTH + RANK:DEPTH + 2 * RANK] = two


def final_kernel(side_ref, core_ref, own_ref, other_ref, f_ref, basis_ref, keep_ref, send_ref):
    upper = side_ref[0] == 1
    for t in range(NT):
        inverse = core_ref[t, :, DEPTH:DEPTH + RANK].astype(F32)
        inverse = inverse + core_ref[t, :, DEPTH + RANK:DEPTH + 2 * RANK].astype(F32)
        total = own_ref[t].astype(F32) + other_ref[t].astype(F32)
        half = jnp.where(upper, total[:, HALF:ROWS], total[:, 0:HALF])
        basis_ref[t] = nn_dot(inverse, half, HIGHEST) * math.sqrt(2048.0)
        part = nn_dot(core_ref[t, :, 0:DEPTH], f_ref[t])
        first, last = part[:, 0:HALF], part[:, HALF:ROWS]
        keep_ref[t] = jnp.where(upper, last, first)
        send_ref[t] = jnp.where(upper, first, last).astype(BF16)


def in_hbm(x):
    return pltpu.with_memory_space_constraint(x, pltpu.HBM)


def local(factors, cores, tile_list, probes):
    swap = [(0, 1), (1, 0)]
    z = lax.axis_index("z").astype(jnp.int32).reshape(1)
    side = lax.axis_index("core").astype(jnp.int32).reshape(1)
    row_first = tile_list[:, 0].astype(jnp.int32)
    row_second = tile_list[:, 1].astype(jnp.int32)
    params = pltpu.CompilerParams(vmem_limit_bytes=32 * 1024 * 1024)

    smem = pl.BlockSpec(memory_space=pltpu.SMEM)
    hbm = pl.BlockSpec(memory_space=pl.ANY)
    vmem = pl.BlockSpec(memory_space=pltpu.VMEM)

    def call(kernel, out_shape, in_specs, *args, scratch=()):
        return pl.pallas_call(
            kernel,
            out_shape=out_shape,
            in_specs=in_specs,
            out_specs=jax.tree.map(lambda _: vmem, out_shape),
            scratch_shapes=scratch,
            compiler_params=params,
        )(*args)

    def shape(*dims, dtype=BF16):
        return jax.ShapeDtypeStruct(dims, dtype)

    def exchange(x):
        return lax.all_to_all(x, "z", 0, 0, tiled=True)

    mine = jnp.transpose(factors[0, 0], (1, 0))
    sliced = pl.pallas_call(
        slice_kernel,
        out_shape=shape(NZ, RANK, ROWS),
        grid=(NZ,),
        in_specs=[pl.BlockSpec((RANK, ROWS), lambda t: (0, t))],
        out_specs=pl.BlockSpec((1, RANK, ROWS), lambda t: (t, 0, 0)),
        compiler_params=params,
    )(mine)
    panels = exchange(sliced).reshape(DEPTH, ROWS)
    gathered = in_hbm(lax.all_gather(panels, ("x", "y"), axis=0, tiled=False))
    core, _ = lax.optimization_barrier((cores[0], panels))
    all_cores = lax.all_gather(core, "z", axis=0, tiled=False)

    probe = in_hbm(jnp.transpose(probes, (1, 2, 0)))
    block = shape(NT, DEPTH, ROWS)
    sketch, left, right = call(
        sketch_kernel,
        (shape(NT, RANK, DEPTH), block, block),
        [smem, smem, smem, hbm, hbm, hbm],
        row_first,
        row_second,
        z,
        gathered,
        probe,
        all_cores,
        scratch=[pltpu.VMEM((NT, RANK, ROWS), BF16)] + [pltpu.SemaphoreType.DMA((NT,))] * 3,
    )
    first = call(first_kernel, shape(NZ, RANK, DEPTH), [vmem] * 2, exchange(sketch), all_cores)
    own = call(sample_kernel, shape(NT, RANK, ROWS), [vmem] * 2, exchange(first), left)
    other = lax.ppermute(own, "core", swap)
    wide = DEPTH + 2 * RANK
    stacked = call(gram_kernel, shape(NT, RANK, wide), [vmem] * 3, own, other, left)
    second = call(second_kernel, shape(NZ, RANK, wide), [vmem] * 2, exchange(stacked), all_cores)
    half = (NT, RANK, HALF)
    basis, keep, send = call(
        final_kernel,
        (shape(*half, dtype=F32), shape(*half, dtype=F32), shape(*half)),
        [smem] + [vmem] * 4,
        side,
        exchange(second),
        own,
        other,
        right,
    )
    update = keep + lax.ppermute(send, "core", swap).astype(F32)
    return jnp.transpose(basis, (2, 0, 1)), jnp.transpose(update, (2, 0, 1))


def solution(mesh):
    fine = Mesh(mesh.devices.reshape(8, 2, 4, 8), ("z", "core", "x", "y"))
    layer, col = ("z", "core"), ("x", "y")
    placed = (
        P(layer, col, None, None),
        P(layer, None, None),
        P(col, None),
        P(None, col, None),
    )
    return jax.shard_map(
        local,
        mesh=fine,
        in_specs=placed,
        out_specs=(P(layer, col, None), P(layer, col, None)),
        check_vma=False,
    )
```

time: 270 us -> 250 us (0.926)
  Pallas kernels: 31.8 us -> 15 us
  blocking collectives: 106 us -> 103 us
    pallas_call x7, Pallas kernels: 31.8 us -> 15 us  [the longest x6 14.8 us: call(): pl.pallas_call(kernel, out_shape=out_shape, in_specs=in_specs, out_specs=...]
    all_to_all x4, blocking collectives: 86.8 us -> 83.9 us  [exchange(): return lax.all_to_all(x, 'z', 0, 0, tiled=True)]
where the time goes in v2:
time: 250 us
  blocking collectives  103 us (41%)
  waiting for transfers between devices  103 us (41%)
  Pallas kernels  15 us (6%)
  between operations  14.1 us (6%)
  starting transfers between devices  11.9 us (5%)
    all_to_all x4, blocking collectives, exchange(): return lax.all_to_all(x, 'z', 0, 0, tiled=True)  83.9 us
    all_gather x1, waiting for transfers between devices, local(): gathered = in_hbm(lax.all_gather(panels, ('x', 'y'), axis=0, tiled=False))  80.1 us
    all_to_all x1, waiting for transfers between devices, exchange(): return lax.all_to_all(x, 'z', 0, 0, tiled=True)  20.7 us
    all_gather x1, blocking collectives, local(): all_cores = lax.all_gather(core, 'z', axis=0, tiled=False)  19.3 us
    pallas_call x6, Pallas kernels, call(): pl.pallas_call(kernel, out_shape=out_shape, in_specs=in_specs, out_specs=...  14.8 us
    ppermute x1, starting transfers between devices, local(): other = lax.ppermute(own, 'core', swap)  5.91 us
  transfers between devices with their start and end apart: 4, of which 4 were waited for; matrix products, arithmetic and copies ran while one was open for 0% of the time, Pallas kernels for 0%

profile of v2, /device:TPU:1, one launch (start us, length us, event | category | flops | bytes accessed | tf_op | source)
XLA Modules:
  0.0 249.6 jit_solution(11478641091631586613)
XLA Ops:
  7.2 0.0 all-gather.3.cloned.1.call-start
  7.2 0.0 copy-start
  7.2 0.9 copy-done
  8.2 0.2 shard_map.59
  8.4 21.3 %all_to_all.25 = bf16[8,64,256]{2,1,0:T(8,128)(2,1)} all-to-all(bf16[8,64,256]{2,1,0:T(8,128)(2,1)S(1)} %shard_map.59), channel_id=1, replica_groups=mesh['z'=8,'core'=2,'x'=4,'y'=8] {'z'}, dimensions={0} | all-to-all | bytes 524288 | tf_op jit(solution)/shard_map/all_to_all | solution.py:221
  29.6 0.0 all-gather.3.cloned.1.call-update
  29.7 19.3 %all-gather = f32[512,64]{1,0:T(8,128)S(1)} all-gather(f32[64,64]{1,0:T(8,128)} %bitcast.22), channel_id=2, replica_groups=mesh['z'=8,'core'=2,'x'=4,'y'=8] {'z'}, dimensions={0}, use_global_device_ids=true | all-gather | bytes 147456 | tf_op jit(solution)/shard_map/all_gather | solution.py:235
  49.0 0.8 slice_bitcast_fusion
  49.7 80.1 %all-gather.3.cloned.1.call-done.f_ref = bf16[32,512,256]{2,1,0:T(8,128)(2,1)} async-done(((bf16[1,512,256]{2,1,0:T(8,128)(2,1)}), bf16[32,512,256]{2,1,0:T(8,128)(2,1)}) %all-gather.3.cloned.1.call-update) | async-done | bytes 8388624 | tf_op jit(solution)/shard_map/all_gather | solution.py:233
  129.8 3.4 %shard_map.60 = (bf16[8,64,512]{2,1,0:T(8,128)(2,1)S(1)}, bf16[8,512,256]{2,1,0:T(8,128)(2,1)S(1)}, bf16[8,512,256]{2,1,0:T(8,128)(2,1)S(1)}) custom-call(s32[8]{0:T(128)S(1)} %get-tuple-element.15.first_ref, s32[8]{0:T(128)S(1)} %get-tuple-element.14.second_ref, s32[1]{0:T(128)} %bitcast.3.z_ref, bf16[32,512,256]{2,1,0:T(8,128)(2,1)} %all-gather.3.cloned.1.call-done.f_ref, ...), custom_call_target="tpu_custom_call" | custom-call | tf_op jit(solution)/shard_map/pallas_call | solution.py:208
  133.2 22.1 %all_to_all.26.part_ref = bf16[8,64,512]{2,1,0:T(8,128)(2,1)S(1)} all-to-all(bf16[8,64,512]{2,1,0:T(8,128)(2,1)S(1)} %get-tuple-element.8), channel_id=1, replica_groups=mesh['z'=8,'core'=2,'x'=4,'y'=8] {'z'}, dimensions={0} | all-to-all | bytes 1048576 | tf_op jit(solution)/shard_map/all_to_all | solution.py:221
  155.3 0.7 shard_map.61
  156.0 17.5 %all_to_all.27.core_ref = bf16[8,64,512]{2,1,0:T(8,128)(2,1)S(1)} all-to-all(bf16[8,64,512]{2,1,0:T(8,128)(2,1)S(1)} %shard_map.61), channel_id=1, replica_groups=mesh['z'=8,'core'=2,'x'=4,'y'=8] {'z'}, dimensions={0} | all-to-all | bytes 1048576 | tf_op jit(solution)/shard_map/all_to_all | solution.py:221
  173.5 0.5 shard_map.62.own_ref
  174.0 5.9 %collective-permute-start = (bf16[8,64,256]{2,1,0:T(8,128)(2,1)S(1)}, bf16[8,64,256]{2,1,0:T(8,128)(2,1)S(1)}, u32[]{:S(2)}, u32[]{:S(2)}) collective-permute-start(bf16[8,64,256]{2,1,0:T(8,128)(2,1)S(1)} %shard_map.62.own_ref), channel_id=1, source_target_pairs={{0,32},{32,0},{1,33},{33,1},{2,34},{34,2},{3,35},{35,3},{4,36},{36... | collective-permute-start | bytes 786440 | tf_op jit(solution)/shard_map/ppermute | solution.py:253
  179.9 1.1 collective-permute-done.other_ref
  181.0 1.4 shard_map.63
  182.5 23.1 %all_to_all.28.part_ref = bf16[8,64,640]{2,1,0:T(8,128)(2,1)S(1)} all-to-all(bf16[8,64,640]{2,1,0:T(8,128)(2,1)S(1)} %shard_map.63), channel_id=1, replica_groups=mesh['z'=8,'core'=2,'x'=4,'y'=8] {'z'}, dimensions={0} | all-to-all | bytes 1310720 | tf_op jit(solution)/shard_map/all_to_all | solution.py:221
  205.6 7.4 %shard_map.64 = bf16[8,64,640]{2,1,0:T(8,128)(2,1)} custom-call(bf16[8,64,640]{2,1,0:T(8,128)(2,1)S(1)} %all_to_all.28.part_ref, f32[8,64,64]{2,1,0:T(8,128)S(1)} %bitcast.18), custom_call_target="tpu_custom_call" | custom-call | tf_op jit(solution)/shard_map/pallas_call | solution.py:208
  213.0 3.5 %all-to-all-start.4 = ((bf16[8,64,640]{2,1,0:T(8,128)(2,1)}), bf16[8,64,640]{2,1,0:T(8,128)(2,1)S(1)}, u32[]{:S(2)}, u32[]{:S(2)}) async-start(bf16[8,64,640]{2,1,0:T(8,128)(2,1)} %shard_map.64), calls=%async_computation.4 | async-start | bytes 1310720 | tf_op jit(solution)/shard_map/all_to_all | solution.py:221
  216.6 20.7 %all-to-all-done.4.core_ref = bf16[8,64,640]{2,1,0:T(8,128)(2,1)S(1)} async-done(((bf16[8,64,640]{2,1,0:T(8,128)(2,1)}), bf16[8,64,640]{2,1,0:T(8,128)(2,1)S(1)}, u32[]{:S(2)}, u32[]{:S(2)}) %all-to-all-start.4) | async-done | bytes 655392 | tf_op jit(solution)/shard_map/all_to_all | solution.py:221
  237.3 1.4 shard_map.65
  238.6 2.4 collective-permute-start.1
  241.0 1.0 collective-permute-done.1
  242.0 0.7 add_bitcast_fusion
Async XLA Ops:
  7.2 122.7 %all-gather.3.cloned.1.call-start = ((), (), s32[]{:S(2)}) async-start(), calls=%async_computation.5 | async-start | bytes 8650752 | tf_op jit(solution)/shard_map/all_gather | solution.py:233
  7.2 1.0 copy-start
  174.0 7.1 %collective-permute-start = (bf16[8,64,256]{2,1,0:T(8,128)(2,1)S(1)}, bf16[8,64,256]{2,1,0:T(8,128)(2,1)S(1)}, u32[]{:S(2)}, u32[]{:S(2)}) collective-permute-start(bf16[8,64,256]{2,1,0:T(8,128)(2,1)S(1)} %shard_map.62.own_ref), channel_id=1, source_target_pairs={{0,32},{32,0},{1,33},{33,1},{2,34},{34,2},{3,35},{35,3},{4,36},{36... | collective-permute-start | bytes 786440 | tf_op jit(solution)/shard_map/ppermute | solution.py:253
  213.0 24.2 %all-to-all-start.4 = ((bf16[8,64,640]{2,1,0:T(8,128)(2,1)}), bf16[8,64,640]{2,1,0:T(8,128)(2,1)S(1)}, u32[]{:S(2)}, u32[]{:S(2)}) async-start(bf16[8,64,640]{2,1,0:T(8,128)(2,1)} %shard_map.64), calls=%async_computation.4 | async-start | bytes 1310720 | tf_op jit(solution)/shard_map/all_to_all | solution.py:221
  238.6 3.4 %collective-permute-start.1 = (bf16[8,64,128]{2,1,0:T(8,128)(2,1)S(1)}, bf16[8,64,128]{2,1,0:T(8,128)(2,1)S(1)}, u32[]{:S(2)}, u32[]{:S(2)}) collective-permute-start(bf16[8,64,128]{2,1,0:T(8,128)(2,1)S(1)} %get-tuple-element.13), channel_id=1, source_target_pairs={{0,32},{32,0},{1,33},{33,1},{2,34},{34,2},{3,35},{35,3},{4,36},{36... | collective-permute-start | bytes 393224 | tf_op jit(solution)/shard_map/ppermute | solution.py:268
Sparse Core Ops, SparseCore 0:
  29.8 100.0 all-gather.2

commit v3 on v2

--- a/solution.py
+++ b/solution.py
@@ -16,6 +16,8 @@
 RANK = 64
 PANELS = 8
 DEPTH = PANELS * RANK
+PART = 128
+MAIN = DEPTH - PART
 ROWS = 256
 HALF = 128
 
@@ -44,27 +46,31 @@
     o_ref[0] = f_ref[...]
 
 
-def sketch_kernel(first_ref, second_ref, z_ref, f_ref, probe_ref, cores_ref, o_ref, left_ref, right_ref,
+def sketch_kernel(first_ref, second_ref, z_ref, f_ref, g_ref, probe_ref, cores_ref, o_ref, left_ref, right_ref,
                   slot_ref, sem_right, sem_left, sem_probe):
     start = pl.multiple_of(z_ref[0] * ROWS, ROWS)
-    rights, probes, lefts = [], [], []
-    for t in range(NT):
-        rights.append(pltpu.make_async_copy(f_ref.at[second_ref[t]], right_ref.at[t], sem_right.at[t]))
-        probes.append(
-            pltpu.make_async_copy(probe_ref.at[t, :, pl.ds(start, ROWS)], slot_ref.at[t], sem_probe.at[t])
+    def fetch(rows_ref, t, out_ref, sem):
+        block = rows_ref[t]
+        return (
+            pltpu.make_async_copy(f_ref.at[block], out_ref.at[t, 0:MAIN], sem.at[t, 0]),
+            pltpu.make_async_copy(g_ref.at[block], out_ref.at[t, MAIN:DEPTH], sem.at[t, 1]),
         )
-        lefts.append(pltpu.make_async_copy(f_ref.at[first_ref[t]], left_ref.at[t], sem_left.at[t]))
-    for t in range(NT):
-        rights[t].start()
-        probes[t].start()
-    for t in range(NT):
-        lefts[t].start()
-    for t in range(NT):
-        rights[t].wait()
-        probes[t].wait()
+
+    rights, lefts = [], []
+    for t in range(NT):
+        probe = pltpu.make_async_copy(probe_ref.at[t, :, pl.ds(start, ROWS)], slot_ref.at[t], sem_probe.at[t])
+        rights.append(fetch(second_ref, t, right_ref, sem_right) + (probe,))
+        lefts.append(fetch(first_ref, t, left_ref, sem_left))
+    for group in rights + lefts:
+        for copy in group:
+            copy.start()
+    for t in range(NT):
+        for copy in rights[t]:
+            copy.wait()
         o_ref[t] = nt_dot(slot_ref[t], right_ref[t]).astype(BF16)
-    for t in range(NT):
-        lefts[t].wait()
+    for group in lefts:
+        for copy in group:
+            copy.wait()
 
 
 def core_products(total, cores_ref):
@@ -230,7 +236,10 @@
         compiler_params=params,
     )(mine)
     panels = exchange(sliced).reshape(DEPTH, ROWS)
-    gathered = in_hbm(lax.all_gather(panels, ("x", "y"), axis=0, tiled=False))
+    col = ("x", "y")
+    gathered = in_hbm(lax.all_gather(panels[:MAIN], col, axis=0, tiled=False))
+    copies = jnp.broadcast_to(panels[MAIN:], (lax.axis_size(col), PART, ROWS))
+    beside = in_hbm(lax.all_to_all(copies, col, 0, 0, tiled=True))
     core, _ = lax.optimization_barrier((cores[0], panels))
     all_cores = lax.all_gather(core, "z", axis=0, tiled=False)
 
@@ -239,14 +248,19 @@
     sketch, left, right = call(
         sketch_kernel,
         (shape(NT, RANK, DEPTH), block, block),
-        [smem, smem, smem, hbm, hbm, hbm],
+        [smem, smem, smem, hbm, hbm, hbm, hbm],
         row_first,
         row_second,
         z,
         gathered,
+        beside,
         probe,
         all_cores,
-        scratch=[pltpu.VMEM((NT, RANK, ROWS), BF16)] + [pltpu.SemaphoreType.DMA((NT,))] * 3,
+        scratch=[pltpu.VMEM((NT, RANK, ROWS), BF16)] + [
+            pltpu.SemaphoreType.DMA((NT, 2)),
+            pltpu.SemaphoreType.DMA((NT, 2)),
+            pltpu.SemaphoreType.DMA((NT,)),
+        ],
     )
     first = call(first_kernel, shape(NZ, RANK, DEPTH), [vmem] * 2, exchange(sketch), all_cores)
     own = call(sample_kernel, shape(NT, RANK, ROWS), [vmem] * 2, exchange(first), left)

time: 250 us -> 250 us (level)
  waiting for transfers between devices: 103 us -> 91.2 us
  starting transfers between devices: 11.9 us -> 22.3 us
    all_gather x1, waiting for transfers between devices: 80.1 us -> 32.6 us  [local(): gathered = in_hbm(lax.all_gather(panels[:MAIN], col, axis=0, tiled=False))]
    all_to_all x0 -> x1, waiting for transfers between devices: none -> 35.8 us  [local(): beside = in_hbm(lax.all_to_all(copies, col, 0, 0, tiled=True))]
    all_to_all x0 -> x1, starting transfers between devices: none -> 9.8 us  [local(): beside = in_hbm(lax.all_to_all(copies, col, 0, 0, tiled=True))]
    all_to_all x4, blocking collectives: 83.9 us -> 81.1 us  [exchange(): return lax.all_to_all(x, 'z', 0, 0, tiled=True)]
  transfers between devices with their start and end apart: 4 -> 5, of which waited for: 4 -> 5; matrix products, arithmetic and copies ran while one was open for 0% -> 1% of each run, Pallas kernels for 0% -> 0%
where the time goes in v3:
time: 250 us; the launch traced here: 249 us
  blocking collectives  102 us (41%)
  waiting for transfers between devices  91.2 us (36%)
  starting transfers between devices  22.3 us (9%)
  Pallas kernels  15.8 us (6%)
  between operations  14.1 us (6%)
  local copies, waits for them, and re-layouts  3.23 us (1%)
    all_to_all x4, blocking collectives, exchange(): return lax.all_to_all(x, 'z', 0, 0, tiled=True)  81.1 us
    all_to_all x1, waiting for transfers between devices, local(): beside = in_hbm(lax.all_to_all(copies, col, 0, 0, tiled=True))  35.8 us
    all_gather x1, waiting for transfers between devices, local(): gathered = in_hbm(lax.all_gather(panels[:MAIN], col, axis=0, tiled=False))  32.6 us
    all_gather x1, blocking collectives, local(): all_cores = lax.all_gather(core, 'z', axis=0, tiled=False)  20.9 us
    all_to_all x1, waiting for transfers between devices, exchange(): return lax.all_to_all(x, 'z', 0, 0, tiled=True)  20.7 us
    pallas_call x6, Pallas kernels, call(): pl.pallas_call(kernel, out_shape=out_shape, in_specs=in_specs, out_specs=...  15.6 us
    all_to_all x1, starting transfers between devices, local(): beside = in_hbm(lax.all_to_all(copies, col, 0, 0, tiled=True))  9.8 us
    ppermute x1, starting transfers between devices, local(): other = lax.ppermute(own, 'core', swap)  6.58 us
  transfers between devices with their start and end apart: 5, of which 5 were waited for; matrix products, arithmetic and copies ran while one was open for 1% of the time, Pallas kernels for 0%

profile of v3, /device:TPU:1, one launch (start us, length us, event | category | flops | bytes accessed | tf_op | source)
XLA Modules:
  0.0 249.4 jit_solution(7413227911067724596)
XLA Ops:
  7.2 0.0 all-gather.3.cloned.1.call-start
  7.2 0.0 copy-start
  7.2 0.9 copy-done
  8.2 0.2 shard_map.59
  8.4 21.1 %all_to_all.30 = bf16[8,64,256]{2,1,0:T(8,128)(2,1)S(1)} all-to-all(bf16[8,64,256]{2,1,0:T(8,128)(2,1)S(1)} %shard_map.59), channel_id=1, replica_groups=mesh['z'=8,'core'=2,'x'=4,'y'=8] {'z'}, dimensions={0} | all-to-all | bytes 524288 | tf_op jit(solution)/shard_map/all_to_all | solution.py:227
  29.5 0.7 slice.21
  30.2 0.0 all-gather.3.cloned.1.call-update
  30.2 1.6 broadcast_in_dim.3
  31.8 0.0 copy-start.2
  31.8 0.0 copy-start.3
  31.8 9.8 %all-to-all-start.1 = ((bf16[32,128,256]{2,1,0:T(8,128)(2,1)}), bf16[32,128,256]{2,1,0:T(8,128)(2,1)S(1)}, u32[]{:S(2)}, u32[]{:S(2)}) async-start(bf16[32,128,256]{2,1,0:T(8,128)(2,1)} %broadcast_in_dim.3), calls=%async_computation.1 | async-start | bytes 4194304 | tf_op jit(solution)/shard_map/all_to_all | solution.py:242
  41.6 0.0 copy-done.2
  41.6 20.9 %all-gather = f32[512,64]{1,0:T(8,128)S(1)} all-gather(f32[64,64]{1,0:T(8,128)S(1)} %bitcast.24), channel_id=2, replica_groups=mesh['z'=8,'core'=2,'x'=4,'y'=8] {'z'}, dimensions={0}, use_global_device_ids=true | all-gather | bytes 147456 | tf_op jit(solution)/shard_map/all_gather | solution.py:244
  62.5 0.0 copy-done.3
  62.6 35.8 %all-to-all-done.1.g_ref = bf16[32,128,256]{2,1,0:T(8,128)(2,1)S(1)} async-done(((bf16[32,128,256]{2,1,0:T(8,128)(2,1)}), bf16[32,128,256]{2,1,0:T(8,128)(2,1)S(1)}, u32[]{:S(2)}, u32[]{:S(2)}) %all-to-all-start.1) | async-done | bytes 2097184 | tf_op jit(solution)/shard_map/all_to_all | solution.py:242
  98.4 0.0 copy-start.1
  98.4 32.6 %all-gather.3.cloned.1.call-done.f_ref = bf16[32,384,256]{2,1,0:T(8,128)(2,1)} async-done(((bf16[1,384,256]{2,1,0:T(8,128)(2,1)}), bf16[32,384,256]{2,1,0:T(8,128)(2,1)}) %all-gather.3.cloned.1.call-update) | async-done | bytes 6291472 | tf_op jit(solution)/shard_map/all_gather | solution.py:240
  130.9 0.0 copy-done.1
  130.9 4.2 %shard_map.60 = (bf16[8,64,512]{2,1,0:T(8,128)(2,1)S(1)}, bf16[8,512,256]{2,1,0:T(8,128)(2,1)S(1)}, bf16[8,512,256]{2,1,0:T(8,128)(2,1)S(1)}) custom-call(s32[8]{0:T(128)S(1)} %get-tuple-element.15.first_ref, s32[8]{0:T(128)S(1)} %get-tuple-element.14.second_ref, s32[1]{0:T(128)} %bitcast.3.z_ref, bf16[32,384,256]{2,1,0:T(8,128)(2,1)} %all-gather.3.cloned.1.call-done.f_ref, ...), custom_call_target="tpu_custom_call" | custom-call | tf_op jit(solution)/shard_map/pallas_call | solution.py:214
  135.2 19.9 %all_to_all.31.part_ref = bf16[8,64,512]{2,1,0:T(8,128)(2,1)S(1)} all-to-all(bf16[8,64,512]{2,1,0:T(8,128)(2,1)S(1)} %get-tuple-element.8), channel_id=1, replica_groups=mesh['z'=8,'core'=2,'x'=4,'y'=8] {'z'}, dimensions={0} | all-to-all | bytes 1048576 | tf_op jit(solution)/shard_map/all_to_all | solution.py:227
  155.1 0.7 shard_map.61
  155.8 16.8 %all_to_all.32.core_ref = bf16[8,64,512]{2,1,0:T(8,128)(2,1)S(1)} all-to-all(bf16[8,64,512]{2,1,0:T(8,128)(2,1)S(1)} %shard_map.61), channel_id=1, replica_groups=mesh['z'=8,'core'=2,'x'=4,'y'=8] {'z'}, dimensions={0} | all-to-all | bytes 1048576 | tf_op jit(solution)/shard_map/all_to_all | solution.py:227
  172.7 0.5 shard_map.62.own_ref
  173.1 6.6 %collective-permute-start = (bf16[8,64,256]{2,1,0:T(8,128)(2,1)S(1)}, bf16[8,64,256]{2,1,0:T(8,128)(2,1)S(1)}, u32[]{:S(2)}, u32[]{:S(2)}) collective-permute-start(bf16[8,64,256]{2,1,0:T(8,128)(2,1)S(1)} %shard_map.62.own_ref), channel_id=1, source_target_pairs={{0,32},{32,0},{1,33},{33,1},{2,34},{34,2},{3,35},{35,3},{4,36},{36... | collective-permute-start | bytes 786440 | tf_op jit(solution)/shard_map/ppermute | solution.py:267
  179.7 1.1 collective-permute-done.other_ref
  180.9 1.4 shard_map.63
  182.3 23.1 %all_to_all.33.part_ref = bf16[8,64,640]{2,1,0:T(8,128)(2,1)S(1)} all-to-all(bf16[8,64,640]{2,1,0:T(8,128)(2,1)S(1)} %shard_map.63), channel_id=1, replica_groups=mesh['z'=8,'core'=2,'x'=4,'y'=8] {'z'}, dimensions={0} | all-to-all | bytes 1310720 | tf_op jit(solution)/shard_map/all_to_all | solution.py:227
  205.4 7.4 %shard_map.64 = bf16[8,64,640]{2,1,0:T(8,128)(2,1)} custom-call(bf16[8,64,640]{2,1,0:T(8,128)(2,1)S(1)} %all_to_all.33.part_ref, f32[8,64,64]{2,1,0:T(8,128)S(1)} %bitcast.19), custom_call_target="tpu_custom_call" | custom-call | tf_op jit(solution)/shard_map/pallas_call | solution.py:214
  212.9 3.5 %all-to-all-start.5 = ((bf16[8,64,640]{2,1,0:T(8,128)(2,1)}), bf16[8,64,640]{2,1,0:T(8,128)(2,1)S(1)}, u32[]{:S(2)}, u32[]{:S(2)}) async-start(bf16[8,64,640]{2,1,0:T(8,128)(2,1)} %shard_map.64), calls=%async_computation.5 | async-start | bytes 1310720 | tf_op jit(solution)/shard_map/all_to_all | solution.py:227
  216.4 20.7 %all-to-all-done.5.core_ref = bf16[8,64,640]{2,1,0:T(8,128)(2,1)S(1)} async-done(((bf16[8,64,640]{2,1,0:T(8,128)(2,1)}), bf16[8,64,640]{2,1,0:T(8,128)(2,1)S(1)}, u32[]{:S(2)}, u32[]{:S(2)}) %all-to-all-start.5) | async-done | bytes 655392 | tf_op jit(solution)/shard_map/all_to_all | solution.py:227
  237.1 1.4 shard_map.65
  238.5 2.4 collective-permute-start.1
  240.9 1.0 collective-permute-done.1
  241.8 0.7 add_bitcast_fusion
  (2 shorter events, 0.0 us)
Async XLA Ops:
  7.2 123.8 %all-gather.3.cloned.1.call-start = ((), (), s32[]{:S(2)}) async-start(), calls=%async_computation.6 | async-start | bytes 6488064 | tf_op jit(solution)/shard_map/all_gather | solution.py:240
  7.2 1.0 copy-start
  31.8 9.8 %copy-start.2 = (f32[1,64,64]{2,1,0:T(8,128)S(1)}, f32[1,64,64]{2,1,0:T(8,128)}, u32[]{:S(2)}) copy-start(f32[1,64,64]{2,1,0:T(8,128)} %param.5) | copy-start | bytes 49156
  31.8 30.7 %copy-start.3 = (s32[8,2]{0,1:T(2,128)S(1)}, s32[8,2]{0,1:T(2,128)}, u32[]{:S(2)}) copy-start(s32[8,2]{0,1:T(2,128)} %param.6) | copy-start | bytes 196
  31.8 66.6 %all-to-all-start.1 = ((bf16[32,128,256]{2,1,0:T(8,128)(2,1)}), bf16[32,128,256]{2,1,0:T(8,128)(2,1)S(1)}, u32[]{:S(2)}, u32[]{:S(2)}) async-start(bf16[32,128,256]{2,1,0:T(8,128)(2,1)} %broadcast_in_dim.3), calls=%async_computation.1 | async-start | bytes 4194304 | tf_op jit(solution)/shard_map/all_to_all | solution.py:242
  98.4 32.6 %copy-start.1 = (bf16[32,128,256]{2,1,0:T(8,128)(2,1)}, bf16[32,128,256]{2,1,0:T(8,128)(2,1)S(1)}, u32[]{:S(2)}) copy-start(bf16[32,128,256]{2,1,0:T(8,128)(2,1)S(1)} %all-to-all-done.1.g_ref) | copy-start | bytes 6291460
  173.1 7.7 %collective-permute-start = (bf16[8,64,256]{2,1,0:T(8,128)(2,1)S(1)}, bf16[8,64,256]{2,1,0:T(8,128)(2,1)S(1)}, u32[]{:S(2)}, u32[]{:S(2)}) collective-permute-start(bf16[8,64,256]{2,1,0:T(8,128)(2,1)S(1)} %shard_map.62.own_ref), channel_id=1, source_target_pairs={{0,32},{32,0},{1,33},{33,1},{2,34},{34,2},{3,35},{35,3},{4,36},{36... | collective-permute-start | bytes 786440 | tf_op jit(solution)/shard_map/ppermute | solution.py:267
  212.9 24.2 %all-to-all-start.5 = ((bf16[8,64,640]{2,1,0:T(8,128)(2,1)}), bf16[8,64,640]{2,1,0:T(8,128)(2,1)S(1)}, u32[]{:S(2)}, u32[]{:S(2)}) async-start(bf16[8,64,640]{2,1,0:T(8,128)(2,1)} %shard_map.64), calls=%async_computation.5 | async-start | bytes 1310720 | tf_op jit(solution)/shard_map/all_to_all | solution.py:227
  238.5 3.4 %collective-permute-start.1 = (bf16[8,64,128]{2,1,0:T(8,128)(2,1)S(1)}, bf16[8,64,128]{2,1,0:T(8,128)(2,1)S(1)}, u32[]{:S(2)}, u32[]{:S(2)}) collective-permute-start(bf16[8,64,128]{2,1,0:T(8,128)(2,1)S(1)} %get-tuple-element.13), channel_id=1, source_target_pairs={{0,32},{32,0},{1,33},{33,1},{2,34},{34,2},{3,35},{35,3},{4,36},{36... | collective-permute-start | bytes 393224 | tf_op jit(solution)/shard_map/ppermute | solution.py:282
Sparse Core Ops, SparseCore 0:
  30.4 100.5 all-gather.2
